TPU v7x, 512 devices: a whole 4x4x16 slice. The times are simulated.
512 devices in a mesh: img: 32 (over y, z_hi, core), view: 16 (over x, z_lo).
Axes of the slice: x: 4, y: 4, z: 16 (z_hi: 4, z_lo: 4; z = z_hi * 4 + z_lo), core: 2. Of those that a mesh axis runs over, the one named last changes fastest.
Arguments:
- images: float32 [2, 12288, 1024], P(None, ('img', 'view')), may hold values from -30 to 30, as said below
- views: float32 [8192, 1024], P('view'), may hold values from -5 to 5, as said below
Outputs:
- new_views: float32 [8192, 1024], P('view')
Inputs may be any that keep to these rules, and one draw needn't show every extreme that they name: `images`: real valued Fourier values. `views`: real valued Fourier values.
All inputs are finite; a program needn't handle non-finite values.
Results may differ from a plain program's by a relative error of at most 0.0003.
Values sent between devices are 32-bit elements; how exact they have to be, the bound alone decides.
No kernel may reach another device: no remote copies, remote signals or barrier semaphores. Data moves between devices by JAX's collectives and lax.ppermute only.
A program may use at most 64 MiB of HBM per device.

v0:
```python
import math

import jax
import jax.numpy as jnp
from jax import lax
from jax.experimental import pallas as pl
from jax.experimental.pallas import tpu as pltpu
from jax.sharding import Mesh, PartitionSpec as P

F = 1024
LANES = 128
BLOCK = 192
HALF = 256
ROWS = 64
AXES = ("y", "zh", "c", "x", "zl")
VIEW = ("x", "zl")
BETA = 1.6 / math.sqrt(F)
SWAP = [(0, 1), (1, 0)]
UP = [(i, (i + 1) % 4) for i in range(4)]
DOWN = [(i, (i - 1) % 4) for i in range(4)]
ACROSS = [(i, (i + 2) % 4) for i in range(4)]
EVEN, ODD = [(0, 1), (2, 3)], [(1, 2), (3, 0)]
CROSS = [[2 * a, 2 * b] for a, b in EVEN] + [[2 * a + 1, 2 * b + 1] for a, b in ODD]
UNCROSS = [[2 * a, 2 * b] for a, b in ODD] + [[2 * a + 1, 2 * b + 1] for a, b in EVEN]
VMEM = pl.BlockSpec(memory_space=pltpu.VMEM)
SMEM = pl.BlockSpec(memory_space=pltpu.SMEM)
BF16, F32 = jnp.bfloat16, jnp.float32


def shape(*dims, dtype=F32):
    return jax.ShapeDtypeStruct(dims, dtype)


def split(x):
    high = x.astype(BF16)
    return high, (x - high.astype(F32)).astype(BF16)


def product(a, b, dims):
    def dot(p, q):
        return lax.dot_general(p, q, (dims, ((), ())), preferred_element_type=F32)

    return dot(a[0], b[0]) + (dot(a[0], b[1]) + dot(a[1], b[0]))


def call(body, out, n_in, flops, smem=0):
    return pl.pallas_call(
        body,
        out_shape=out,
        in_specs=[SMEM] * smem + [VMEM] * n_in,
        out_specs=jax.tree.map(lambda _: VMEM, out),
        cost_estimate=pl.CostEstimate(flops=flops, bytes_accessed=4 << 20, transcendentals=0),
        compiler_params=pltpu.CompilerParams(vmem_limit_bytes=16 << 20),
    )


def prepare_body(views, high, low, norm):
    v = views[...]
    high[...], low[...] = split(v)
    norm[...] = jnp.broadcast_to(0.5 * jnp.sum(v * v, axis=1, keepdims=True), norm.shape)


def score(views, images, e, stats, high, low):
    pair = split(images[...])
    high[...], low[...] = pair
    dots = product((views[0][...], views[1][...]), pair, ((1,), (1,)))
    s = BETA * (dots - views[2][:, :1])
    peak = jnp.max(s, axis=0, keepdims=True)
    expo = jnp.exp(s - peak)
    e[...] = expo
    stats[...] = jnp.concatenate([peak, jnp.sum(expo, axis=0, keepdims=True)], axis=0)


def block_out(v):
    return [shape(v, BLOCK), shape(2, BLOCK), shape(BLOCK, F, dtype=BF16), shape(BLOCK, F, dtype=BF16)]


def some_body(*refs):
    views, n = refs[:3], (len(refs) - 3) // 5
    blocks, outs = refs[3 : 3 + n], refs[3 + n :]
    for k in range(n):
        score(views, blocks[k], *outs[4 * k : 4 * k + 4])


def some(prepared, blocks):
    v, n = prepared[0].shape[0], len(blocks)
    got = call(some_body, block_out(v) * n, 3 + n, 6 * n * BLOCK * v * F)(*prepared, *blocks)
    return [got[k : k + 4] for k in range(0, len(got), 4)]


def rest_body(where, *refs):
    views, blocks, known, outs, every = refs[:3], refs[3:5], refs[5:7], refs[7:15], refs[15]
    for k in range(2):
        score(views, blocks[k], *outs[4 * k : 4 * k + 4])
    for o, s in enumerate((known[0], outs[1], known[1], outs[5])):
        line = lax.rem(where[0] + o, 4)
        for k in range(16):
            every[k, line] = s[...]


def rest(where, prepared, blocks, stats):
    v = prepared[0].shape[0]
    out = block_out(v) * 2 + [shape(16, 4, 2, BLOCK)]
    got = call(rest_body, out, 7, 12 * BLOCK * v * F, smem=1)(where, *prepared, *blocks, *stats)
    return got[:4], got[4:8], got[8]


def numerator_body(own, where, every, *refs):
    out = refs[-1]
    core = where[1] if own else 1 - where[1]
    start = pl.multiple_of(core * HALF, HALF)
    acc = jnp.zeros((HALF, F), F32)
    mass = jnp.zeros((HALF, 1), F32)
    for o in range(4):
        e, local, high, low = refs[4 * o : 4 * o + 4]
        stats = every[:, lax.rem(where[0] + o, 4)]
        maxes, sums = stats[:, 0], stats[:, 1]
        peak = jnp.max(maxes, axis=0, keepdims=True)
        total = jnp.sum(sums * jnp.exp(maxes - peak), axis=0, keepdims=True)
        w = e[pl.ds(start, HALF), :] * (jnp.exp(local[0:1] - peak) / total)
        mass = mass + jnp.sum(w, axis=1, keepdims=True)
        acc = acc + product(split(w), (high[...], low[...]), ((1,), (0,)))
    lane = lax.broadcasted_iota(jnp.int32, (8, LANES), 1) // 16
    for y in range(4):
        held = jnp.zeros((8, LANES), F32)
        for r in range(8):
            row = y * ROWS + r * 8
            for t in range(8):
                out[y, r * 8 + t] = acc[row : row + 8, t * LANES : (t + 1) * LANES]
            held = jnp.where(lane == r, mass[row : row + 8], held)
        out[y, ROWS] = held


def numerator(own, where, every, blocks):
    flat = [a for block in blocks for a in block]
    body = lambda *refs: numerator_body(own, *refs)
    out = shape(4, ROWS + 1, 8, LANES)
    return call(body, out, 1 + len(flat), 24 * HALF * BLOCK * F, smem=1)(where, every, *flat)


def gather_body(parts, out):
    out[...] = (parts[0] + parts[1]) + (parts[2] + parts[3])


def gather(parts):
    return call(gather_body, shape(ROWS + 1, 8, LANES), 1, 4 * ROWS * F)(parts)


def update_body(where, views, sums, out):
    start = pl.multiple_of(where[2], ROWS)
    mass = sums[0, ROWS] + sums[1, ROWS] + 1.0
    for r in range(8):
        scale = mass[:, 16 * r : 16 * r + 1]
        for t in range(8):
            k = r * 8 + t
            here = views[pl.ds(start + r * 8, 8), t * LANES : (t + 1) * LANES]
            new = (here + (sums[0, k] + sums[1, k])) / scale
            for y in range(4):
                out[y, k] = new


def update(*args):
    return call(update_body, shape(4, ROWS, 8, LANES), 2, 4 * ROWS * F, smem=1)(*args)


def em_round(images, views):
    core, y, x = lax.axis_index("c"), lax.axis_index("y"), lax.axis_index("x")
    n_views = views.shape[0]
    images, core, x, row, lower = lax.optimization_barrier((images, core, x, core * HALF + y * ROWS, core == 0))
    where = jnp.stack([x, core, row]).astype(jnp.int32)
    rows = images.reshape(-1, F)
    across = lax.ppermute(rows, "x", ACROSS)
    own = lax.all_gather(rows, "zl", axis=0, tiled=True)
    up = lax.ppermute(own, "x", UP)
    down = lax.ppermute(own, "x", DOWN)
    across, own = lax.optimization_barrier((across, own))
    far = lax.all_gather(across, "zl", axis=0, tiled=True)
    prepared = call(
        prepare_body,
        [shape(n_views, F, dtype=BF16), shape(n_views, F, dtype=BF16), shape(n_views, LANES)],
        1, 4 * n_views * F,
    )(views)
    b_own, b_far = some(prepared, (own, far))
    b_down, b_up, every = rest(where, prepared, (down, up), (b_own[1], b_far[1]))
    every = lax.all_to_all(every, VIEW, 0, 0)
    blocks = (b_own, b_down, b_far, b_up)
    theirs = lax.ppermute(numerator(False, where, every, blocks), "c", SWAP)
    mine = numerator(True, where, every, blocks) + theirs
    sums = gather(lax.all_to_all(mine, "y", 0, 0))
    pair = lax.all_gather(sums, ("zh", "c"), axis=0, axis_index_groups=CROSS)
    sums = lax.all_gather(pair[0] + pair[1], ("zh", "c"), axis=0, axis_index_groups=UNCROSS)
    new = update(where, views, sums)
    new = lax.all_to_all(new, "y", 0, 0)
    other = lax.ppermute(new, "c", SWAP)
    both = jnp.where(lower, jnp.stack([new, other]), jnp.stack([other, new]))
    return both.reshape(n_views // 8, 8, 8, LANES).transpose(0, 2, 1, 3).reshape(n_views, F)


def solution(mesh):
    inner = Mesh(mesh.devices.reshape(4, 4, 2, 4, 4), AXES)
    placed = (P(None, AXES, None), P(VIEW, None))
    return jax.shard_map(em_round, mesh=inner, in_specs=placed, out_specs=P(VIEW, None), check_vma=False)
```

profile of v0, /device:TPU:1, one launch (start us, length us, event | category | flops | bytes accessed | tf_op | source)
XLA Modules:
  0.0 173.3 jit_solution(6031998596980524144)
XLA Ops:
  0.0 19.4 %all_gather.16.refs_3_ = f32[192,1024]{1,0:T(8,128)S(1)} all-gather(f32[48,1024]{1,0:T(8,128)} %bitcast.15), channel_id=1, replica_groups=mesh['y'=4,'zh'=4,'c'=2,'x'=4,'zl'=4] {'zl'}, dimensions={0}, use_global_device_ids=true | all-gather | bytes 983040 | tf_op jit(solution)/shard_map/all_gather | solution.py:173
  19.4 2.9 %collective-permute-start.1 = (f32[192,1024]{1,0:T(8,128)S(1)}, f32[192,1024]{1,0:T(8,128)S(1)}, u32[]{:S(2)}, u32[]{:S(2)}) collective-permute-start(f32[192,1024]{1,0:T(8,128)S(1)} %all_gather.16.refs_3_), channel_id=1, source_target_pairs={{0,4},{4,8},{8,12},{12,0},{1,5},{5,9},{9,13},{13,1},{2,6},{6,10},{... | collective-permute-start | bytes 2359304 | tf_op jit(solution)/shard_map/ppermute | solution.py:174
  22.4 3.6 %collective-permute-start = (f32[192,1024]{1,0:T(8,128)S(1)}, f32[192,1024]{1,0:T(8,128)S(1)}, u32[]{:S(2)}, u32[]{:S(2)}) collective-permute-start(f32[192,1024]{1,0:T(8,128)S(1)} %all_gather.16.refs_3_), channel_id=1, source_target_pairs={{0,12},{4,0},{8,4},{12,8},{1,13},{5,1},{9,5},{13,9},{2,14},{6,2},{... | collective-permute-start | bytes 2359304 | tf_op jit(solution)/shard_map/ppermute | solution.py:175
  25.9 3.3 %collective-permute-start.2 = (f32[48,1024]{1,0:T(8,128)}, f32[48,1024]{1,0:T(8,128)S(1)}, u32[]{:S(2)}, u32[]{:S(2)}) collective-permute-start(f32[48,1024]{1,0:T(8,128)} %bitcast.16), channel_id=1, source_target_pairs={{0,8},{4,12},{8,0},{12,4},{1,9},{5,13},{9,1},{13,5},{2,10},{6,14},... | collective-permute-start | bytes 589832 | tf_op jit(solution)/shard_map/ppermute | solution.py:172
  29.2 0.0 copy-start
  29.2 1.6 copy-done
  30.8 0.5 shard_map.28
  31.3 0.1 pad_add_fusion.where.refs_0_
  31.3 11.7 %collective-permute-done.2 = f32[48,1024]{1,0:T(8,128)S(1)} collective-permute-done((f32[48,1024]{1,0:T(8,128)}, f32[48,1024]{1,0:T(8,128)S(1)}, u32[]{:S(2)}, u32[]{:S(2)}) %collective-permute-start.2) | collective-permute-done | bytes 196640 | tf_op jit(solution)/shard_map/ppermute | solution.py:172
  43.1 16.2 %all_gather.17.refs_4_ = f32[192,1024]{1,0:T(8,128)S(1)} all-gather(f32[48,1024]{1,0:T(8,128)S(1)} %collective-permute-done.2), channel_id=1, replica_groups=mesh['y'=4,'zh'=4,'c'=2,'x'=4,'zl'=4] {'zl'}, dimensions={0}, use_global_device_ids=true | all-gather | bytes 983040 | tf_op jit(solution)/shard_map/all_gather | solution.py:177
  59.3 2.1 %shard_map.29 = (f32[512,192]{1,0:T(8,128)S(1)}, f32[2,192]{1,0:T(2,128)S(1)}, bf16[192,1024]{1,0:T(8,128)(2,1)S(1)}, bf16[192,1024]{1,0:T(8,128)(2,1)S(1)}, f32...) custom-call(bf16[512,1024]{1,0:T(8,128)(2,1)S(1)} %get-tuple-element., ...), custom_call_target="tpu_custom_call" | custom-call | flops 1207959552 | bytes 4194304 | tf_op jit(solution)/shard_map/pallas_call | solution.py:87
  61.4 0.0 collective-permute-done.1.refs_4_
  61.4 0.0 collective-permute-done.refs_3_
  61.4 2.6 %shard_map.30 = (f32[512,192]{1,0:T(8,128)S(1)}, f32[2,192]{1,0:T(2,128)S(1)}, bf16[192,1024]{1,0:T(8,128)(2,1)S(1)}, bf16[192,1024]{1,0:T(8,128)(2,1)S(1)}, f32...) custom-call(s32[3]{0:T(128)S(1)} %pad_add_fusion.where.refs_0_, ...), custom_call_target="tpu_custom_call" | custom-call | flops 1207959552 | bytes 4194304 | tf_op jit(solution)/shard_map/pallas_call | solution.py:104
  64.0 13.7 %all_to_all.15.refs_1_ = f32[16,4,2,192]{3,2,1,0:T(2,128)S(1)} all-to-all(f32[16,4,2,192]{3,2,1,0:T(2,128)S(1)} %get-tuple-element.44), channel_id=1, replica_groups=mesh['y'=4,'zh'=4,'c'=2,'x'=4,'zl'=4] {'x','zl'}, dimensions={0} | all-to-all | bytes 196608 | tf_op jit(solution)/shard_map/all_to_all | solution.py:185
  77.7 2.4 %shard_map.32 = f32[4,65,8,128]{3,2,1,0:T(8,128)S(1)} custom-call(s32[3]{0:T(128)S(1)} %pad_add_fusion.where.refs_0_, f32[16,4,2,192]{3,2,1,0:T(2,128)S(1)} %all_to_all.15.refs_1_, f32[512,192]{1,0:T(8,128)S(1)} %get-tuple-element.45.refs_2_, f32[2,192]{1,0:T(2,128)S(1)} %get-tuple-element.42.refs_5_.refs_3_, ...), custom_call_target="tpu_custom_call" | custom-call | flops 1207959552 | bytes 4194304 | tf_op jit(solution)/shard_map/pallas_call | solution.py:138
  80.1 8.7 %collective-permute-start.3 = (f32[4,65,8,128]{3,2,1,0:T(8,128)S(1)}, f32[4,65,8,128]{3,2,1,0:T(8,128)S(1)}, u32[]{:S(2)}, u32[]{:S(2)}) collective-permute-start(f32[4,65,8,128]{3,2,1,0:T(8,128)S(1)} %shard_map.32), channel_id=1, source_target_pairs={{0,16},{16,0},{1,17},{17,1},{2,18},{18,2},{3,19},{19,3},{4,20},{20... | collective-permute-start | bytes 3194888 | tf_op jit(solution)/shard_map/ppermute | solution.py:187
  88.8 2.4 %shard_map.31 = f32[4,65,8,128]{3,2,1,0:T(8,128)S(1)} custom-call(s32[3]{0:T(128)S(1)} %pad_add_fusion.where.refs_0_, f32[16,4,2,192]{3,2,1,0:T(2,128)S(1)} %all_to_all.15.refs_1_, f32[512,192]{1,0:T(8,128)S(1)} %get-tuple-element.45.refs_2_, f32[2,192]{1,0:T(2,128)S(1)} %get-tuple-element.42.refs_5_.refs_3_, ...), custom_call_target="tpu_custom_call" | custom-call | flops 1207959552 | bytes 4194304 | tf_op jit(solution)/shard_map/pallas_call | solution.py:138
  91.2 0.0 collective-permute-done.3
  91.2 0.1 add.11
  91.4 19.2 %all_to_all.16.parts = f32[4,65,8,128]{3,2,1,0:T(8,128)S(1)} all-to-all(f32[4,65,8,128]{3,2,1,0:T(8,128)S(1)} %add.11), channel_id=1, replica_groups=mesh['y'=4,'zh'=4,'c'=2,'x'=4,'zl'=4] {'y'}, dimensions={0} | all-to-all | bytes 2129920 | tf_op jit(solution)/shard_map/all_to_all | solution.py:189
  110.6 0.0 copy-start.1
  110.7 20.6 %all-gather = f32[130,8,128]{2,1,0:T(8,128)S(1)} all-gather(f32[65,8,128]{2,1,0:T(8,128)S(1)} %shard_map.33), channel_id=2, replica_groups={{0,32},{64,96},{48,80},{112,16},{1,33},{65,97},{49,81},{113,17},{2,34},..., dimensions={0}, use_global_device_ids=true | all-gather | bytes 798720 | tf_op jit(solution)/shard_map/all_gather | solution.py:190
  131.3 17.1 %all-gather.1 = f32[130,8,128]{2,1,0:T(8,128)S(1)} all-gather(f32[65,8,128]{2,1,0:T(8,128)S(1)} %slice_add_fusion), channel_id=3, replica_groups={{32,64},{96,0},{16,48},{80,112},{33,65},{97,1},{17,49},{81,113},{34,66}..., dimensions={0}, use_global_device_ids=true | all-gather | bytes 798720 | tf_op jit(solution)/shard_map/all_gather | solution.py:191
  148.4 0.0 copy-done.1
  148.4 0.7 shard_map.34
  149.1 15.9 %all_to_all.17 = f32[4,64,8,128]{3,2,1,0:T(8,128)S(1)} all-to-all(f32[4,64,8,128]{3,2,1,0:T(8,128)S(1)} %shard_map.34), channel_id=1, replica_groups=mesh['y'=4,'zh'=4,'c'=2,'x'=4,'zl'=4] {'y'}, dimensions={0} | all-to-all | bytes 2097152 | tf_op jit(solution)/shard_map/all_to_all | solution.py:193
  165.0 4.5 %collective-permute-start.4 = (f32[4,64,8,128]{3,2,1,0:T(8,128)S(1)}, f32[4,64,8,128]{3,2,1,0:T(8,128)S(1)}, u32[]{:S(2)}, u32[]{:S(2)}) collective-permute-start(f32[4,64,8,128]{3,2,1,0:T(8,128)S(1)} %all_to_all.17), channel_id=1, source_target_pairs={{0,16},{16,0},{1,17},{17,1},{2,18},{18,2},{3,19},{19,3},{4,20},{20... | collective-permute-start | bytes 3145736 | tf_op jit(solution)/shard_map/ppermute | solution.py:194
  169.5 2.3 %collective-permute-done.4 = f32[4,64,8,128]{3,2,1,0:T(8,128)S(1)} collective-permute-done((f32[4,64,8,128]{3,2,1,0:T(8,128)S(1)}, f32[4,64,8,128]{3,2,1,0:T(8,128)S(1)}, u32[]{:S(2)}, u32[]{:S(2)}) %collective-permute-start.4) | collective-permute-done | bytes 1048608 | tf_op jit(solution)/shard_map/ppermute | solution.py:194
  171.8 1.5 maximum_select_fusion
  (2 shorter events, 0.1 us)
Async XLA Ops:
  19.4 41.9 %collective-permute-start.1 = (f32[192,1024]{1,0:T(8,128)S(1)}, f32[192,1024]{1,0:T(8,128)S(1)}, u32[]{:S(2)}, u32[]{:S(2)}) collective-permute-start(f32[192,1024]{1,0:T(8,128)S(1)} %all_gather.16.refs_3_), channel_id=1, source_target_pairs={{0,4},{4,8},{8,12},{12,0},{1,5},{5,9},{9,13},{13,1},{2,6},{6,10},{... | collective-permute-start | bytes 2359304 | tf_op jit(solution)/shard_map/ppermute | solution.py:174
  22.4 39.0 %collective-permute-start = (f32[192,1024]{1,0:T(8,128)S(1)}, f32[192,1024]{1,0:T(8,128)S(1)}, u32[]{:S(2)}, u32[]{:S(2)}) collective-permute-start(f32[192,1024]{1,0:T(8,128)S(1)} %all_gather.16.refs_3_), channel_id=1, source_target_pairs={{0,12},{4,0},{8,4},{12,8},{1,13},{5,1},{9,5},{13,9},{2,14},{6,2},{... | collective-permute-start | bytes 2359304 | tf_op jit(solution)/shard_map/ppermute | solution.py:175
  25.9 17.1 %collective-permute-start.2 = (f32[48,1024]{1,0:T(8,128)}, f32[48,1024]{1,0:T(8,128)S(1)}, u32[]{:S(2)}, u32[]{:S(2)}) collective-permute-start(f32[48,1024]{1,0:T(8,128)} %bitcast.16), channel_id=1, source_target_pairs={{0,8},{4,12},{8,0},{12,4},{1,9},{5,13},{9,1},{13,5},{2,10},{6,14},... | collective-permute-start | bytes 589832 | tf_op jit(solution)/shard_map/ppermute | solution.py:172
  29.2 1.6 copy-start
  80.1 11.1 %collective-permute-start.3 = (f32[4,65,8,128]{3,2,1,0:T(8,128)S(1)}, f32[4,65,8,128]{3,2,1,0:T(8,128)S(1)}, u32[]{:S(2)}, u32[]{:S(2)}) collective-permute-start(f32[4,65,8,128]{3,2,1,0:T(8,128)S(1)} %shard_map.32), channel_id=1, source_target_pairs={{0,16},{16,0},{1,17},{17,1},{2,18},{18,2},{3,19},{19,3},{4,20},{20... | collective-permute-start | bytes 3194888 | tf_op jit(solution)/shard_map/ppermute | solution.py:187
  110.6 37.8 %copy-start.1 = (f32[512,1024]{1,0:T(8,128)S(1)}, f32[512,1024]{1,0:T(8,128)}, u32[]{:S(2)}) copy-start(f32[512,1024]{1,0:T(8,128)} %views.3) | copy-start | bytes 6291460
  165.0 6.8 %collective-permute-start.4 = (f32[4,64,8,128]{3,2,1,0:T(8,128)S(1)}, f32[4,64,8,128]{3,2,1,0:T(8,128)S(1)}, u32[]{:S(2)}, u32[]{:S(2)}) collective-permute-start(f32[4,64,8,128]{3,2,1,0:T(8,128)S(1)} %all_to_all.17), channel_id=1, source_target_pairs={{0,16},{16,0},{1,17},{17,1},{2,18},{18,2},{3,19},{19,3},{4,20},{20... | collective-permute-start | bytes 3145736 | tf_op jit(solution)/shard_map/ppermute | solution.py:194
where the time goes:
time: 174 us; the launch traced here: 173 us
  blocking collectives  122 us (70%)
  starting transfers between devices  23 us (13%)
  waiting for transfers between devices  14 us (8%)
  Pallas kernels  10.7 us (6%)
  other arithmetic  1.74 us (1%)
    all_gather x1, blocking collectives, em_round(): pair = lax.all_gather(sums, ('zh', 'c'), axis=0, axis_index_groups=CROSS)  20.6 us
    all_gather x1, blocking collectives, em_round(): own = lax.all_gather(rows, 'zl', axis=0, tiled=True)  19.4 us
    all_to_all x1, blocking collectives, em_round(): sums = gather(lax.all_to_all(mine, 'y', 0, 0))  19.2 us
    all_gather x1, blocking collectives, em_round(): lax.all_gather(pair[0] + pair[1], ('zh', 'c'), axis=0, axis_index_groups=...  17.1 us
    all_gather x1, blocking collectives, em_round(): far = lax.all_gather(across, 'zl', axis=0, tiled=True)  16.2 us
    all_to_all x1, blocking collectives, em_round(): new = lax.all_to_all(new, 'y', 0, 0)  15.9 us
    all_to_all x1, blocking collectives, em_round(): every = lax.all_to_all(every, VIEW, 0, 0)  13.7 us
    ppermute x1, waiting for transfers between devices, em_round(): across = lax.ppermute(rows, 'x', ACROSS)  11.7 us
  transfers between devices with their start and end apart: 5, of which 2 were waited for; matrix products, arithmetic and copies ran while one was open for 0% of the time, Pallas kernels for 3%

commit v1 on v0

--- a/solution.py
+++ b/solution.py
@@ -54,17 +54,16 @@
     )
 
 
-def prepare_body(views, high, low, norm):
-    v = views[...]
-    high[...], low[...] = split(v)
-    norm[...] = jnp.broadcast_to(0.5 * jnp.sum(v * v, axis=1, keepdims=True), norm.shape)
-
-
-def score(views, images, e, stats, high, low):
+def half_norm(high, low):
+    v = high[...].astype(F32) + low[...].astype(F32)
+    return 0.5 * jnp.sum(v * v, axis=1, keepdims=True)
+
+
+def score(views, norm, images, e, stats, high, low):
     pair = split(images[...])
     high[...], low[...] = pair
     dots = product((views[0][...], views[1][...]), pair, ((1,), (1,)))
-    s = BETA * (dots - views[2][:, :1])
+    s = BETA * (dots - norm)
     peak = jnp.max(s, axis=0, keepdims=True)
     expo = jnp.exp(s - peak)
     e[...] = expo
@@ -76,22 +75,24 @@
 
 
 def some_body(*refs):
-    views, n = refs[:3], (len(refs) - 3) // 5
-    blocks, outs = refs[3 : 3 + n], refs[3 + n :]
+    views, n = refs[:2], (len(refs) - 2) // 5
+    blocks, outs = refs[2 : 2 + n], refs[2 + n :]
+    norm = half_norm(*views)
     for k in range(n):
-        score(views, blocks[k], *outs[4 * k : 4 * k + 4])
+        score(views, norm, blocks[k], *outs[4 * k : 4 * k + 4])
 
 
 def some(prepared, blocks):
     v, n = prepared[0].shape[0], len(blocks)
-    got = call(some_body, block_out(v) * n, 3 + n, 6 * n * BLOCK * v * F)(*prepared, *blocks)
+    got = call(some_body, block_out(v) * n, 2 + n, 6 * n * BLOCK * v * F)(*prepared, *blocks)
     return [got[k : k + 4] for k in range(0, len(got), 4)]
 
 
 def rest_body(where, *refs):
-    views, blocks, known, outs, every = refs[:3], refs[3:5], refs[5:7], refs[7:15], refs[15]
+    views, blocks, known, outs, every = refs[:2], refs[2:4], refs[4:6], refs[6:14], refs[14]
+    norm = half_norm(*views)
     for k in range(2):
-        score(views, blocks[k], *outs[4 * k : 4 * k + 4])
+        score(views, norm, blocks[k], *outs[4 * k : 4 * k + 4])
     for o, s in enumerate((known[0], outs[1], known[1], outs[5])):
         line = lax.rem(where[0] + o, 4)
         for k in range(16):
@@ -101,7 +102,7 @@
 def rest(where, prepared, blocks, stats):
     v = prepared[0].shape[0]
     out = block_out(v) * 2 + [shape(16, 4, 2, BLOCK)]
-    got = call(rest_body, out, 7, 12 * BLOCK * v * F, smem=1)(where, *prepared, *blocks, *stats)
+    got = call(rest_body, out, 6, 12 * BLOCK * v * F, smem=1)(where, *prepared, *blocks, *stats)
     return got[:4], got[4:8], got[8]
 
 
@@ -175,11 +176,8 @@
     down = lax.ppermute(own, "x", DOWN)
     across, own = lax.optimization_barrier((across, own))
     far = lax.all_gather(across, "zl", axis=0, tiled=True)
-    prepared = call(
-        prepare_body,
-        [shape(n_views, F, dtype=BF16), shape(n_views, F, dtype=BF16), shape(n_views, LANES)],
-        1, 4 * n_views * F,
-    )(views)
+    high = lax.reduce_precision(views, 8, 7)
+    prepared = (high.astype(BF16), (views - high).astype(BF16))
     b_own, b_far = some(prepared, (own, far))
     b_down, b_up, every = rest(where, prepared, (down, up), (b_own[1], b_far[1]))
     every = lax.all_to_all(every, VIEW, 0, 0)

time: 174 us -> 159 us (0.914)
  waiting for transfers between devices: 14 us -> 2.28 us
  blocking collectives: 122 us -> 116 us
  starting transfers between devices: 23 us -> 26.3 us
  other arithmetic: 1.74 us -> 3.73 us
    ppermute x1, waiting for transfers between devices: 11.7 us -> 0.01 us  [em_round(): across = lax.ppermute(rows, 'x', ACROSS)]
    all_to_all x1, blocking collectives: 13.7 us -> 9.82 us  [em_round(): every = lax.all_to_all(every, VIEW, 0, 0)]
    ppermute x1, starting transfers between devices: 3.27 us -> 5.46 us  [em_round(): across = lax.ppermute(rows, 'x', ACROSS)]
    convert_element_type x0 -> x1, other arithmetic: none -> 2.02 us  [em_round(): prepared = (high.astype(BF16), (views - high).astype(BF16))]
    all_gather x1, blocking collectives: 19.4 us -> 17.7 us  [em_round(): own = lax.all_gather(rows, 'zl', axis=0, tiled=True)]
    pallas_call x3 -> x2, Pallas kernels: 5.18 us -> 5.09 us  [the longest x1 2.81 us: rest(): call(rest_body, out, 6, 12 * BLOCK * v * F, smem=1)]
  transfers between devices with their start and end apart: 5 -> 5, of which waited for: 2 -> 1; matrix products, arithmetic and copies ran while one was open for 0% -> 1% of each run, Pallas kernels for 3% -> 3%
where the time goes in v1:
time: 159 us
  blocking collectives  116 us (73%)
  starting transfers between devices  26.3 us (17%)
  Pallas kernels  10.6 us (7%)
  other arithmetic  3.73 us (2%)
  waiting for transfers between devices  2.28 us (1%)
    all_gather x1, blocking collectives, em_round(): pair = lax.all_gather(sums, ('zh', 'c'), axis=0, axis_index_groups=CROSS)  20.5 us
    all_to_all x1, blocking collectives, em_round(): sums = gather(lax.all_to_all(mine, 'y', 0, 0))  18.3 us
    all_gather x1, blocking collectives, em_round(): own = lax.all_gather(rows, 'zl', axis=0, tiled=True)  17.7 us
    all_gather x1, blocking collectives, em_round(): lax.all_gather(pair[0] + pair[1], ('zh', 'c'), axis=0, axis_index_groups=...  17.2 us
    all_gather x1, blocking collectives, em_round(): far = lax.all_gather(across, 'zl', axis=0, tiled=True)  16.5 us
    all_to_all x1, blocking collectives, em_round(): new = lax.all_to_all(new, 'y', 0, 0)  15.9 us
    ppermute x1, starting transfers between devices, em_round(): theirs = lax.ppermute(numerator(False, where, every, blocks), 'c', SWAP)  9.88 us
    all_to_all x1, blocking collectives, em_round(): every = lax.all_to_all(every, VIEW, 0, 0)  9.82 us
  transfers between devices with their start and end apart: 5, of which 1 were waited for; matrix products, arithmetic and copies ran while one was open for 1% of the time, Pallas kernels for 3%

profile of v1, /device:TPU:1, one launch (start us, length us, event | category | flops | bytes accessed | tf_op | source)
XLA Modules:
  0.0 158.8 jit_solution(314892132687552195)
XLA Ops:
  0.0 5.5 %collective-permute-start.2 = (f32[48,1024]{1,0:T(8,128)}, f32[48,1024]{1,0:T(8,128)S(1)}, u32[]{:S(2)}, u32[]{:S(2)}) collective-permute-start(f32[48,1024]{1,0:T(8,128)} %bitcast.15), channel_id=1, source_target_pairs={{0,8},{4,12},{8,0},{12,4},{1,9},{5,13},{9,1},{13,5},{2,10},{6,14},... | collective-permute-start | bytes 589832 | tf_op jit(solution)/shard_map/ppermute | solution.py:173
  5.5 17.7 %all_gather.16.refs_2_ = f32[192,1024]{1,0:T(8,128)S(1)} all-gather(f32[48,1024]{1,0:T(8,128)} %bitcast.16), channel_id=1, replica_groups=mesh['y'=4,'zh'=4,'c'=2,'x'=4,'zl'=4] {'zl'}, dimensions={0}, use_global_device_ids=true | all-gather | bytes 983040 | tf_op jit(solution)/shard_map/all_gather | solution.py:174
  23.1 2.2 %collective-permute-start.1 = (f32[192,1024]{1,0:T(8,128)S(1)}, f32[192,1024]{1,0:T(8,128)S(1)}, u32[]{:S(2)}, u32[]{:S(2)}) collective-permute-start(f32[192,1024]{1,0:T(8,128)S(1)} %all_gather.16.refs_2_), channel_id=1, source_target_pairs={{0,4},{4,8},{8,12},{12,0},{1,5},{5,9},{9,13},{13,1},{2,6},{6,10},{... | collective-permute-start | bytes 2359304 | tf_op jit(solution)/shard_map/ppermute | solution.py:175
  25.3 4.3 %collective-permute-start = (f32[192,1024]{1,0:T(8,128)S(1)}, f32[192,1024]{1,0:T(8,128)S(1)}, u32[]{:S(2)}, u32[]{:S(2)}) collective-permute-start(f32[192,1024]{1,0:T(8,128)S(1)} %all_gather.16.refs_2_), channel_id=1, source_target_pairs={{0,12},{4,0},{8,4},{12,8},{1,13},{5,1},{9,5},{13,9},{2,14},{6,2},{... | collective-permute-start | bytes 2359304 | tf_op jit(solution)/shard_map/ppermute | solution.py:176
  29.6 2.0 %fusion = (bf16[512,1024]{1,0:T(8,128)(2,1)S(1)}, bf16[512,1024]{1,0:T(8,128)(2,1)S(1)}) fusion(f32[512,1024]{1,0:T(8,128)} %views.1), kind=kLoop, calls=%fused_computation.2 | loop fusion | flops 2097152 | bytes 4194304 | tf_op jit(solution)/shard_map/convert_element_type | solution.py:180
  31.6 0.1 pad_add_fusion.where.refs_0_
  31.7 0.0 collective-permute-done.2
  31.7 16.5 %all_gather.17.refs_3_ = f32[192,1024]{1,0:T(8,128)S(1)} all-gather(f32[48,1024]{1,0:T(8,128)S(1)} %collective-permute-done.2), channel_id=1, replica_groups=mesh['y'=4,'zh'=4,'c'=2,'x'=4,'zl'=4] {'zl'}, dimensions={0}, use_global_device_ids=true | all-gather | bytes 983040 | tf_op jit(solution)/shard_map/all_gather | solution.py:178
  48.2 2.3 %shard_map.28 = (f32[512,192]{1,0:T(8,128)S(1)}, f32[2,192]{1,0:T(2,128)S(1)}, bf16[192,1024]{1,0:T(8,128)(2,1)S(1)}, bf16[192,1024]{1,0:T(8,128)(2,1)S(1)}, f32...) custom-call(bf16[512,1024]{1,0:T(8,128)(2,1)S(1)} %get-tuple-element., ...), custom_call_target="tpu_custom_call" | custom-call | flops 1207959552 | bytes 4194304 | tf_op jit(solution)/shard_map/pallas_call | solution.py:87
  50.5 0.0 collective-permute-done.1.refs_3_
  50.5 0.0 collective-permute-done.refs_2_
  50.5 2.8 %shard_map.29 = (f32[512,192]{1,0:T(8,128)S(1)}, f32[2,192]{1,0:T(2,128)S(1)}, bf16[192,1024]{1,0:T(8,128)(2,1)S(1)}, bf16[192,1024]{1,0:T(8,128)(2,1)S(1)}, f32...) custom-call(s32[3]{0:T(128)S(1)} %pad_add_fusion.where.refs_0_, ...), custom_call_target="tpu_custom_call" | custom-call | flops 1207959552 | bytes 4194304 | tf_op jit(solution)/shard_map/pallas_call | solution.py:105
  53.3 9.8 %all_to_all.15.refs_1_ = f32[16,4,2,192]{3,2,1,0:T(2,128)S(1)} all-to-all(f32[16,4,2,192]{3,2,1,0:T(2,128)S(1)} %get-tuple-element.38), channel_id=1, replica_groups=mesh['y'=4,'zh'=4,'c'=2,'x'=4,'zl'=4] {'x','zl'}, dimensions={0} | all-to-all | bytes 196608 | tf_op jit(solution)/shard_map/all_to_all | solution.py:183
  63.1 2.4 %shard_map.31 = f32[4,65,8,128]{3,2,1,0:T(8,128)S(1)} custom-call(s32[3]{0:T(128)S(1)} %pad_add_fusion.where.refs_0_, f32[16,4,2,192]{3,2,1,0:T(2,128)S(1)} %all_to_all.15.refs_1_, f32[512,192]{1,0:T(8,128)S(1)} %get-tuple-element.39.refs_2_, f32[2,192]{1,0:T(2,128)S(1)} %get-tuple-element.36.refs_4_.refs_3_, ...), custom_call_target="tpu_custom_call" | custom-call | flops 1207959552 | bytes 4194304 | tf_op jit(solution)/shard_map/pallas_call | solution.py:139
  65.5 9.9 %collective-permute-start.3 = (f32[4,65,8,128]{3,2,1,0:T(8,128)S(1)}, f32[4,65,8,128]{3,2,1,0:T(8,128)S(1)}, u32[]{:S(2)}, u32[]{:S(2)}) collective-permute-start(f32[4,65,8,128]{3,2,1,0:T(8,128)S(1)} %shard_map.31), channel_id=1, source_target_pairs={{0,16},{16,0},{1,17},{17,1},{2,18},{18,2},{3,19},{19,3},{4,20},{20... | collective-permute-start | bytes 3194888 | tf_op jit(solution)/shard_map/ppermute | solution.py:185
  75.4 2.4 %shard_map.30 = f32[4,65,8,128]{3,2,1,0:T(8,128)S(1)} custom-call(s32[3]{0:T(128)S(1)} %pad_add_fusion.where.refs_0_, f32[16,4,2,192]{3,2,1,0:T(2,128)S(1)} %all_to_all.15.refs_1_, f32[512,192]{1,0:T(8,128)S(1)} %get-tuple-element.39.refs_2_, f32[2,192]{1,0:T(2,128)S(1)} %get-tuple-element.36.refs_4_.refs_3_, ...), custom_call_target="tpu_custom_call" | custom-call | flops 1207959552 | bytes 4194304 | tf_op jit(solution)/shard_map/pallas_call | solution.py:139
  77.8 0.0 collective-permute-done.3
  77.8 0.1 add.11
  77.9 18.3 %all_to_all.16.parts = f32[4,65,8,128]{3,2,1,0:T(8,128)S(1)} all-to-all(f32[4,65,8,128]{3,2,1,0:T(8,128)S(1)} %add.11), channel_id=1, replica_groups=mesh['y'=4,'zh'=4,'c'=2,'x'=4,'zl'=4] {'y'}, dimensions={0} | all-to-all | bytes 2129920 | tf_op jit(solution)/shard_map/all_to_all | solution.py:187
  96.2 0.0 copy-start
  96.2 20.5 %all-gather = f32[130,8,128]{2,1,0:T(8,128)S(1)} all-gather(f32[65,8,128]{2,1,0:T(8,128)S(1)} %shard_map.32), channel_id=2, replica_groups={{0,32},{64,96},{48,80},{112,16},{1,33},{65,97},{49,81},{113,17},{2,34},..., dimensions={0}, use_global_device_ids=true | all-gather | bytes 798720 | tf_op jit(solution)/shard_map/all_gather | solution.py:188
  116.8 17.2 %all-gather.1 = f32[130,8,128]{2,1,0:T(8,128)S(1)} all-gather(f32[65,8,128]{2,1,0:T(8,128)S(1)} %slice_add_fusion), channel_id=3, replica_groups={{32,64},{96,0},{16,48},{80,112},{33,65},{97,1},{17,49},{81,113},{34,66}..., dimensions={0}, use_global_device_ids=true | all-gather | bytes 798720 | tf_op jit(solution)/shard_map/all_gather | solution.py:189
  133.9 0.0 copy-done
  133.9 0.7 shard_map.33
  134.6 15.9 %all_to_all.17 = f32[4,64,8,128]{3,2,1,0:T(8,128)S(1)} all-to-all(f32[4,64,8,128]{3,2,1,0:T(8,128)S(1)} %shard_map.33), channel_id=1, replica_groups=mesh['y'=4,'zh'=4,'c'=2,'x'=4,'zl'=4] {'y'}, dimensions={0} | all-to-all | bytes 2097152 | tf_op jit(solution)/shard_map/all_to_all | solution.py:191
  150.5 4.5 %collective-permute-start.4 = (f32[4,64,8,128]{3,2,1,0:T(8,128)S(1)}, f32[4,64,8,128]{3,2,1,0:T(8,128)S(1)}, u32[]{:S(2)}, u32[]{:S(2)}) collective-permute-start(f32[4,64,8,128]{3,2,1,0:T(8,128)S(1)} %all_to_all.17), channel_id=1, source_target_pairs={{0,16},{16,0},{1,17},{17,1},{2,18},{18,2},{3,19},{19,3},{4,20},{20... | collective-permute-start | bytes 3145736 | tf_op jit(solution)/shard_map/ppermute | solution.py:192
  155.0 2.3 %collective-permute-done.4 = f32[4,64,8,128]{3,2,1,0:T(8,128)S(1)} collective-permute-done((f32[4,64,8,128]{3,2,1,0:T(8,128)S(1)}, f32[4,64,8,128]{3,2,1,0:T(8,128)S(1)}, u32[]{:S(2)}, u32[]{:S(2)}) %collective-permute-start.4) | collective-permute-done | bytes 1048608 | tf_op jit(solution)/shard_map/ppermute | solution.py:192
  157.3 1.5 maximum_select_fusion
  (2 shorter events, 0.1 us)
Async XLA Ops:
  0.0 31.7 %collective-permute-start.2 = (f32[48,1024]{1,0:T(8,128)}, f32[48,1024]{1,0:T(8,128)S(1)}, u32[]{:S(2)}, u32[]{:S(2)}) collective-permute-start(f32[48,1024]{1,0:T(8,128)} %bitcast.15), channel_id=1, source_target_pairs={{0,8},{4,12},{8,0},{12,4},{1,9},{5,13},{9,1},{13,5},{2,10},{6,14},... | collective-permute-start | bytes 589832 | tf_op jit(solution)/shard_map/ppermute | solution.py:173
  23.1 27.4 %collective-permute-start.1 = (f32[192,1024]{1,0:T(8,128)S(1)}, f32[192,1024]{1,0:T(8,128)S(1)}, u32[]{:S(2)}, u32[]{:S(2)}) collective-permute-start(f32[192,1024]{1,0:T(8,128)S(1)} %all_gather.16.refs_2_), channel_id=1, source_target_pairs={{0,4},{4,8},{8,12},{12,0},{1,5},{5,9},{9,13},{13,1},{2,6},{6,10},{... | collective-permute-start | bytes 2359304 | tf_op jit(solution)/shard_map/ppermute | solution.py:175
  25.3 25.2 %collective-permute-start = (f32[192,1024]{1,0:T(8,128)S(1)}, f32[192,1024]{1,0:T(8,128)S(1)}, u32[]{:S(2)}, u32[]{:S(2)}) collective-permute-start(f32[192,1024]{1,0:T(8,128)S(1)} %all_gather.16.refs_2_), channel_id=1, source_target_pairs={{0,12},{4,0},{8,4},{12,8},{1,13},{5,1},{9,5},{13,9},{2,14},{6,2},{... | collective-permute-start | bytes 2359304 | tf_op jit(solution)/shard_map/ppermute | solution.py:176
  65.5 12.3 %collective-permute-start.3 = (f32[4,65,8,128]{3,2,1,0:T(8,128)S(1)}, f32[4,65,8,128]{3,2,1,0:T(8,128)S(1)}, u32[]{:S(2)}, u32[]{:S(2)}) collective-permute-start(f32[4,65,8,128]{3,2,1,0:T(8,128)S(1)} %shard_map.31), channel_id=1, source_target_pairs={{0,16},{16,0},{1,17},{17,1},{2,18},{18,2},{3,19},{19,3},{4,20},{20... | collective-permute-start | bytes 3194888 | tf_op jit(solution)/shard_map/ppermute | solution.py:185
  96.2 37.8 %copy-start = (f32[512,1024]{1,0:T(8,128)S(1)}, f32[512,1024]{1,0:T(8,128)}, u32[]{:S(2)}) copy-start(f32[512,1024]{1,0:T(8,128)} %views.1) | copy-start | bytes 6291460
  150.5 6.8 %collective-permute-start.4 = (f32[4,64,8,128]{3,2,1,0:T(8,128)S(1)}, f32[4,64,8,128]{3,2,1,0:T(8,128)S(1)}, u32[]{:S(2)}, u32[]{:S(2)}) collective-permute-start(f32[4,64,8,128]{3,2,1,0:T(8,128)S(1)} %all_to_all.17), channel_id=1, source_target_pairs={{0,16},{16,0},{1,17},{17,1},{2,18},{18,2},{3,19},{19,3},{4,20},{20... | collective-permute-start | bytes 3145736 | tf_op jit(solution)/shard_map/ppermute | solution.py:192

commit v2 on v0

--- a/solution.py
+++ b/solution.py
@@ -105,19 +105,27 @@
     return got[:4], got[4:8], got[8]
 
 
-def numerator_body(own, where, every, *refs):
-    out = refs[-1]
+def numerator_body(own, where, *refs):
+    if own:
+        factors, blocks, out = refs[0], refs[1:-1], refs[-1]
+    else:
+        every, blocks, out, factors = refs[0], refs[1:-2], refs[-2], refs[-1]
     core = where[1] if own else 1 - where[1]
     start = pl.multiple_of(core * HALF, HALF)
     acc = jnp.zeros((HALF, F), F32)
     mass = jnp.zeros((HALF, 1), F32)
     for o in range(4):
-        e, local, high, low = refs[4 * o : 4 * o + 4]
-        stats = every[:, lax.rem(where[0] + o, 4)]
-        maxes, sums = stats[:, 0], stats[:, 1]
-        peak = jnp.max(maxes, axis=0, keepdims=True)
-        total = jnp.sum(sums * jnp.exp(maxes - peak), axis=0, keepdims=True)
-        w = e[pl.ds(start, HALF), :] * (jnp.exp(local[0:1] - peak) / total)
+        e, local, high, low = blocks[4 * o : 4 * o + 4]
+        if own:
+            factor = factors[o : o + 1]
+        else:
+            stats = every[:, lax.rem(where[0] + o, 4)]
+            maxes, sums = stats[:, 0], stats[:, 1]
+            peak = jnp.max(maxes, axis=0, keepdims=True)
+            total = jnp.sum(sums * jnp.exp(maxes - peak), axis=0, keepdims=True)
+            factor = jnp.exp(local[0:1] - peak) / total
+            factors[o : o + 1] = factor
+        w = e[pl.ds(start, HALF), :] * factor
         mass = mass + jnp.sum(w, axis=1, keepdims=True)
         acc = acc + product(split(w), (high[...], low[...]), ((1,), (0,)))
     lane = lax.broadcasted_iota(jnp.int32, (8, LANES), 1) // 16
@@ -131,11 +139,20 @@
         out[y, ROWS] = held
 
 
-def numerator(own, where, every, blocks):
+def numerator(own, where, lead, blocks):
     flat = [a for block in blocks for a in block]
     body = lambda *refs: numerator_body(own, *refs)
-    out = shape(4, ROWS + 1, 8, LANES)
-    return call(body, out, 1 + len(flat), 24 * HALF * BLOCK * F, smem=1)(where, every, *flat)
+    out = [shape(4, ROWS + 1, 8, LANES)] + ([] if own else [shape(4, BLOCK)])
+    got = call(body, out, 1 + len(flat), 24 * HALF * BLOCK * F, smem=1)(where, lead, *flat)
+    return got[0] if own else got
+
+
+def both_body(pair, out):
+    out[...] = pair[0] + pair[1]
+
+
+def both_of(pair):
+    return call(both_body, shape(*pair.shape[1:]), 1, ROWS * F)(pair)
 
 
 def gather_body(parts, out):
@@ -184,11 +201,12 @@
     b_down, b_up, every = rest(where, prepared, (down, up), (b_own[1], b_far[1]))
     every = lax.all_to_all(every, VIEW, 0, 0)
     blocks = (b_own, b_down, b_far, b_up)
-    theirs = lax.ppermute(numerator(False, where, every, blocks), "c", SWAP)
-    mine = numerator(True, where, every, blocks) + theirs
+    theirs, factors = numerator(False, where, every, blocks)
+    theirs = lax.ppermute(theirs, "c", SWAP)
+    mine = numerator(True, where, factors, blocks) + theirs
     sums = gather(lax.all_to_all(mine, "y", 0, 0))
     pair = lax.all_gather(sums, ("zh", "c"), axis=0, axis_index_groups=CROSS)
-    sums = lax.all_gather(pair[0] + pair[1], ("zh", "c"), axis=0, axis_index_groups=UNCROSS)
+    sums = lax.all_gather(both_of(pair), ("zh", "c"), axis=0, axis_index_groups=UNCROSS)
     new = update(where, views, sums)
     new = lax.all_to_all(new, "y", 0, 0)
     other = lax.ppermute(new, "c", SWAP)

time: 174 us -> 174 us (level)
  no operation moved by 1% of the time
where the time goes in v2:
time: 174 us; the launch traced here: 173 us
  blocking collectives  122 us (70%)
  starting transfers between devices  23 us (13%)
  waiting for transfers between devices  14 us (8%)
  Pallas kernels  10.6 us (6%)
    all_gather x1, blocking collectives, em_round(): pair = lax.all_gather(sums, ('zh', 'c'), axis=0, axis_index_groups=CROSS)  20.6 us
    all_gather x1, blocking collectives, em_round(): own = lax.all_gather(rows, 'zl', axis=0, tiled=True)  19.4 us
    all_to_all x1, blocking collectives, em_round(): sums = gather(lax.all_to_all(mine, 'y', 0, 0))  19.2 us
    all_gather x1, blocking collectives, em_round(): lax.all_gather(both_of(pair), ('zh', 'c'), axis=0, axis_index_groups=UNCR...  17.1 us
    all_gather x1, blocking collectives, em_round(): far = lax.all_gather(across, 'zl', axis=0, tiled=True)  16.2 us
    all_to_all x1, blocking collectives, em_round(): new = lax.all_to_all(new, 'y', 0, 0)  15.8 us
    all_to_all x1, blocking collectives, em_round(): every = lax.all_to_all(every, VIEW, 0, 0)  13.7 us
    ppermute x1, waiting for transfers between devices, em_round(): across = lax.ppermute(rows, 'x', ACROSS)  11.7 us
  transfers between devices with their start and end apart: 5, of which 2 were waited for; matrix products, arithmetic and copies ran while one was open for 0% of the time, Pallas kernels for 3%

profile of v2, /device:TPU:1, one launch (start us, length us, event | category | flops | bytes accessed | tf_op | source)
XLA Modules:
  0.0 173.2 jit_solution(842442882814085533)
XLA Ops:
  0.0 19.4 %all_gather.18.refs_3_ = f32[192,1024]{1,0:T(8,128)S(1)} all-gather(f32[48,1024]{1,0:T(8,128)} %bitcast.17), channel_id=1, replica_groups=mesh['y'=4,'zh'=4,'c'=2,'x'=4,'zl'=4] {'zl'}, dimensions={0}, use_global_device_ids=true | all-gather | bytes 983040 | tf_op jit(solution)/shard_map/all_gather | solution.py:190
  19.4 2.9 %collective-permute-start.1 = (f32[192,1024]{1,0:T(8,128)S(1)}, f32[192,1024]{1,0:T(8,128)S(1)}, u32[]{:S(2)}, u32[]{:S(2)}) collective-permute-start(f32[192,1024]{1,0:T(8,128)S(1)} %all_gather.18.refs_3_), channel_id=1, source_target_pairs={{0,4},{4,8},{8,12},{12,0},{1,5},{5,9},{9,13},{13,1},{2,6},{6,10},{... | collective-permute-start | bytes 2359304 | tf_op jit(solution)/shard_map/ppermute | solution.py:191
  22.4 3.6 %collective-permute-start = (f32[192,1024]{1,0:T(8,128)S(1)}, f32[192,1024]{1,0:T(8,128)S(1)}, u32[]{:S(2)}, u32[]{:S(2)}) collective-permute-start(f32[192,1024]{1,0:T(8,128)S(1)} %all_gather.18.refs_3_), channel_id=1, source_target_pairs={{0,12},{4,0},{8,4},{12,8},{1,13},{5,1},{9,5},{13,9},{2,14},{6,2},{... | collective-permute-start | bytes 2359304 | tf_op jit(solution)/shard_map/ppermute | solution.py:192
  25.9 3.3 %collective-permute-start.2 = (f32[48,1024]{1,0:T(8,128)}, f32[48,1024]{1,0:T(8,128)S(1)}, u32[]{:S(2)}, u32[]{:S(2)}) collective-permute-start(f32[48,1024]{1,0:T(8,128)} %bitcast.18), channel_id=1, source_target_pairs={{0,8},{4,12},{8,0},{12,4},{1,9},{5,13},{9,1},{13,5},{2,10},{6,14},... | collective-permute-start | bytes 589832 | tf_op jit(solution)/shard_map/ppermute | solution.py:189
  29.2 0.0 copy-start
  29.2 1.6 copy-done
  30.8 0.5 shard_map.28
  31.3 0.1 pad_add_fusion.where.refs_0_
  31.3 11.7 %collective-permute-done.2 = f32[48,1024]{1,0:T(8,128)S(1)} collective-permute-done((f32[48,1024]{1,0:T(8,128)}, f32[48,1024]{1,0:T(8,128)S(1)}, u32[]{:S(2)}, u32[]{:S(2)}) %collective-permute-start.2) | collective-permute-done | bytes 196640 | tf_op jit(solution)/shard_map/ppermute | solution.py:189
  43.1 16.2 %all_gather.19.refs_4_ = f32[192,1024]{1,0:T(8,128)S(1)} all-gather(f32[48,1024]{1,0:T(8,128)S(1)} %collective-permute-done.2), channel_id=1, replica_groups=mesh['y'=4,'zh'=4,'c'=2,'x'=4,'zl'=4] {'zl'}, dimensions={0}, use_global_device_ids=true | all-gather | bytes 983040 | tf_op jit(solution)/shard_map/all_gather | solution.py:194
  59.3 2.1 %shard_map.29 = (f32[512,192]{1,0:T(8,128)S(1)}, f32[2,192]{1,0:T(2,128)S(1)}, bf16[192,1024]{1,0:T(8,128)(2,1)S(1)}, bf16[192,1024]{1,0:T(8,128)(2,1)S(1)}, f32...) custom-call(bf16[512,1024]{1,0:T(8,128)(2,1)S(1)} %get-tuple-element., ...), custom_call_target="tpu_custom_call" | custom-call | flops 1207959552 | bytes 4194304 | tf_op jit(solution)/shard_map/pallas_call | solution.py:87
  61.4 0.0 collective-permute-done.1.refs_4_
  61.4 0.0 collective-permute-done.refs_3_
  61.4 2.6 %shard_map.30 = (f32[512,192]{1,0:T(8,128)S(1)}, f32[2,192]{1,0:T(2,128)S(1)}, bf16[192,1024]{1,0:T(8,128)(2,1)S(1)}, bf16[192,1024]{1,0:T(8,128)(2,1)S(1)}, f32...) custom-call(s32[3]{0:T(128)S(1)} %pad_add_fusion.where.refs_0_, ...), custom_call_target="tpu_custom_call" | custom-call | flops 1207959552 | bytes 4194304 | tf_op jit(solution)/shard_map/pallas_call | solution.py:104
  64.0 13.7 %all_to_all.15.refs_1_ = f32[16,4,2,192]{3,2,1,0:T(2,128)S(1)} all-to-all(f32[16,4,2,192]{3,2,1,0:T(2,128)S(1)} %get-tuple-element.46), channel_id=1, replica_groups=mesh['y'=4,'zh'=4,'c'=2,'x'=4,'zl'=4] {'x','zl'}, dimensions={0} | all-to-all | bytes 196608 | tf_op jit(solution)/shard_map/all_to_all | solution.py:202
  77.7 2.4 %shard_map.31 = (f32[4,65,8,128]{3,2,1,0:T(8,128)S(1)}, f32[4,192]{1,0:T(4,128)S(1)}) custom-call(s32[3]{0:T(128)S(1)} %pad_add_fusion.where.refs_0_, f32[16,4,2,192]{3,2,1,0:T(2,128)S(1)} %all_to_all.15.refs_1_, f32[512,192]{1,0:T(8,128)S(1)} %get-tuple-element.47.refs_2_, f32[2,192]{1,0:T(2,128)S(1)} %get-tuple-element.44.refs_5_.refs_3_, ...), custom_call_target="tpu_custom_call" | custom-call | flops 1207959552 | bytes 4194304 | tf_op jit(solution)/shard_map/pallas_call | solution.py:146
  80.1 8.7 %collective-permute-start.3 = (f32[4,65,8,128]{3,2,1,0:T(8,128)S(1)}, f32[4,65,8,128]{3,2,1,0:T(8,128)S(1)}, u32[]{:S(2)}, u32[]{:S(2)}) collective-permute-start(f32[4,65,8,128]{3,2,1,0:T(8,128)S(1)} %get-tuple-element.62), channel_id=1, source_target_pairs={{0,16},{16,0},{1,17},{17,1},{2,18},{18,2},{3,19},{19,3},{4,20},{20... | collective-permute-start | bytes 3194888 | tf_op jit(solution)/shard_map/ppermute | solution.py:205
  88.8 2.3 %shard_map.32 = f32[4,65,8,128]{3,2,1,0:T(8,128)S(1)} custom-call(s32[3]{0:T(128)S(1)} %pad_add_fusion.where.refs_0_, f32[4,192]{1,0:T(4,128)S(1)} %get-tuple-element.61.refs_1_, f32[512,192]{1,0:T(8,128)S(1)} %get-tuple-element.47.refs_2_, f32[2,192]{1,0:T(2,128)S(1)} %get-tuple-element.44.refs_5_.refs_3_, bf16[192,1024]{1,0:T(8,128)(2,1)S(1)} %get-tuple-element.48.refs_4_, ...), custom_call_target="tpu_custom_call" | custom-call | flops 1207959552 | bytes 4194304 | tf_op jit(solution)/shard_map/pallas_call | solution.py:146
  91.2 0.0 collective-permute-done.3
  91.2 0.1 add.7
  91.3 19.2 %all_to_all.16.parts = f32[4,65,8,128]{3,2,1,0:T(8,128)S(1)} all-to-all(f32[4,65,8,128]{3,2,1,0:T(8,128)S(1)} %add.7), channel_id=1, replica_groups=mesh['y'=4,'zh'=4,'c'=2,'x'=4,'zl'=4] {'y'}, dimensions={0} | all-to-all | bytes 2129920 | tf_op jit(solution)/shard_map/all_to_all | solution.py:207
  110.5 0.0 copy-start.1
  110.6 20.6 %all-gather = f32[130,8,128]{2,1,0:T(8,128)S(1)} all-gather(f32[65,8,128]{2,1,0:T(8,128)S(1)} %shard_map.33), channel_id=2, replica_groups={{0,32},{64,96},{48,80},{112,16},{1,33},{65,97},{49,81},{113,17},{2,34},..., dimensions={0}, use_global_device_ids=true | all-gather | bytes 798720 | tf_op jit(solution)/shard_map/all_gather | solution.py:208
  131.2 17.1 %all-gather.1 = f32[130,8,128]{2,1,0:T(8,128)S(1)} all-gather(f32[65,8,128]{2,1,0:T(8,128)S(1)} %shard_map.34), channel_id=3, replica_groups={{32,64},{96,0},{16,48},{80,112},{33,65},{97,1},{17,49},{81,113},{34,66}..., dimensions={0}, use_global_device_ids=true | all-gather | bytes 798720 | tf_op jit(solution)/shard_map/all_gather | solution.py:209
  148.3 0.0 copy-done.1
  148.3 0.7 shard_map.35
  149.0 15.8 %all_to_all.17 = f32[4,64,8,128]{3,2,1,0:T(8,128)S(1)} all-to-all(f32[4,64,8,128]{3,2,1,0:T(8,128)S(1)} %shard_map.35), channel_id=1, replica_groups=mesh['y'=4,'zh'=4,'c'=2,'x'=4,'zl'=4] {'y'}, dimensions={0} | all-to-all | bytes 2097152 | tf_op jit(solution)/shard_map/all_to_all | solution.py:211
  164.9 4.5 %collective-permute-start.4 = (f32[4,64,8,128]{3,2,1,0:T(8,128)S(1)}, f32[4,64,8,128]{3,2,1,0:T(8,128)S(1)}, u32[]{:S(2)}, u32[]{:S(2)}) collective-permute-start(f32[4,64,8,128]{3,2,1,0:T(8,128)S(1)} %all_to_all.17), channel_id=1, source_target_pairs={{0,16},{16,0},{1,17},{17,1},{2,18},{18,2},{3,19},{19,3},{4,20},{20... | collective-permute-start | bytes 3145736 | tf_op jit(solution)/shard_map/ppermute | solution.py:212
  169.4 2.3 %collective-permute-done.4 = f32[4,64,8,128]{3,2,1,0:T(8,128)S(1)} collective-permute-done((f32[4,64,8,128]{3,2,1,0:T(8,128)S(1)}, f32[4,64,8,128]{3,2,1,0:T(8,128)S(1)}, u32[]{:S(2)}, u32[]{:S(2)}) %collective-permute-start.4) | collective-permute-done | bytes 1048608 | tf_op jit(solution)/shard_map/ppermute | solution.py:212
  171.7 1.5 maximum_select_fusion
  (2 shorter events, 0.1 us)
Async XLA Ops:
  19.4 41.9 %collective-permute-start.1 = (f32[192,1024]{1,0:T(8,128)S(1)}, f32[192,1024]{1,0:T(8,128)S(1)}, u32[]{:S(2)}, u32[]{:S(2)}) collective-permute-start(f32[192,1024]{1,0:T(8,128)S(1)} %all_gather.18.refs_3_), channel_id=1, source_target_pairs={{0,4},{4,8},{8,12},{12,0},{1,5},{5,9},{9,13},{13,1},{2,6},{6,10},{... | collective-permute-start | bytes 2359304 | tf_op jit(solution)/shard_map/ppermute | solution.py:191
  22.4 39.0 %collective-permute-start = (f32[192,1024]{1,0:T(8,128)S(1)}, f32[192,1024]{1,0:T(8,128)S(1)}, u32[]{:S(2)}, u32[]{:S(2)}) collective-permute-start(f32[192,1024]{1,0:T(8,128)S(1)} %all_gather.18.refs_3_), channel_id=1, source_target_pairs={{0,12},{4,0},{8,4},{12,8},{1,13},{5,1},{9,5},{13,9},{2,14},{6,2},{... | collective-permute-start | bytes 2359304 | tf_op jit(solution)/shard_map/ppermute | solution.py:192
  25.9 17.1 %collective-permute-start.2 = (f32[48,1024]{1,0:T(8,128)}, f32[48,1024]{1,0:T(8,128)S(1)}, u32[]{:S(2)}, u32[]{:S(2)}) collective-permute-start(f32[48,1024]{1,0:T(8,128)} %bitcast.18), channel_id=1, source_target_pairs={{0,8},{4,12},{8,0},{12,4},{1,9},{5,13},{9,1},{13,5},{2,10},{6,14},... | collective-permute-start | bytes 589832 | tf_op jit(solution)/shard_map/ppermute | solution.py:189
  29.2 1.6 copy-start
  80.1 11.1 %collective-permute-start.3 = (f32[4,65,8,128]{3,2,1,0:T(8,128)S(1)}, f32[4,65,8,128]{3,2,1,0:T(8,128)S(1)}, u32[]{:S(2)}, u32[]{:S(2)}) collective-permute-start(f32[4,65,8,128]{3,2,1,0:T(8,128)S(1)} %get-tuple-element.62), channel_id=1, source_target_pairs={{0,16},{16,0},{1,17},{17,1},{2,18},{18,2},{3,19},{19,3},{4,20},{20... | collective-permute-start | bytes 3194888 | tf_op jit(solution)/shard_map/ppermute | solution.py:205
  110.5 37.8 %copy-start.1 = (f32[512,1024]{1,0:T(8,128)S(1)}, f32[512,1024]{1,0:T(8,128)}, u32[]{:S(2)}) copy-start(f32[512,1024]{1,0:T(8,128)} %views.3) | copy-start | bytes 6291460
  164.9 6.8 %collective-permute-start.4 = (f32[4,64,8,128]{3,2,1,0:T(8,128)S(1)}, f32[4,64,8,128]{3,2,1,0:T(8,128)S(1)}, u32[]{:S(2)}, u32[]{:S(2)}) collective-permute-start(f32[4,64,8,128]{3,2,1,0:T(8,128)S(1)} %all_to_all.17), channel_id=1, source_target_pairs={{0,16},{16,0},{1,17},{17,1},{2,18},{18,2},{3,19},{19,3},{4,20},{20... | collective-permute-start | bytes 3145736 | tf_op jit(solution)/shard_map/ppermute | solution.py:212

commit v3 on v2

--- a/solution.py
+++ b/solution.py
@@ -165,13 +165,13 @@
 
 def update_body(where, views, sums, out):
     start = pl.multiple_of(where[2], ROWS)
-    mass = sums[0, ROWS] + sums[1, ROWS] + 1.0
+    inverse = 1.0 / (sums[0, ROWS] + sums[1, ROWS] + 1.0)
     for r in range(8):
-        scale = mass[:, 16 * r : 16 * r + 1]
+        scale = inverse[:, 16 * r : 16 * r + 1]
         for t in range(8):
             k = r * 8 + t
             here = views[pl.ds(start + r * 8, 8), t * LANES : (t + 1) * LANES]
-            new = (here + (sums[0, k] + sums[1, k])) / scale
+            new = (here + (sums[0, k] + sums[1, k])) * scale
             for y in range(4):
                 out[y, k] = new
 

time: 174 us -> 174 us (level)
  no operation moved by 1% of the time
where the time goes in v3:
time: 174 us; the launch traced here: 173 us
  blocking collectives  122 us (70%)
  starting transfers between devices  23 us (13%)
  waiting for transfers between devices  14 us (8%)
  Pallas kernels  10.6 us (6%)
    all_gather x1, blocking collectives, em_round(): pair = lax.all_gather(sums, ('zh', 'c'), axis=0, axis_index_groups=CROSS)  20.6 us
    all_gather x1, blocking collectives, em_round(): own = lax.all_gather(rows, 'zl', axis=0, tiled=True)  19.4 us
    all_to_all x1, blocking collectives, em_round(): sums = gather(lax.all_to_all(mine, 'y', 0, 0))  19.2 us
    all_gather x1, blocking collectives, em_round(): lax.all_gather(both_of(pair), ('zh', 'c'), axis=0, axis_index_groups=UNCR...  17.1 us
    all_gather x1, blocking collectives, em_round(): far = lax.all_gather(across, 'zl', axis=0, tiled=True)  16.2 us
    all_to_all x1, blocking collectives, em_round(): new = lax.all_to_all(new, 'y', 0, 0)  15.8 us
    all_to_all x1, blocking collectives, em_round(): every = lax.all_to_all(every, VIEW, 0, 0)  13.7 us
    ppermute x1, waiting for transfers between devices, em_round(): across = lax.ppermute(rows, 'x', ACROSS)  11.7 us
  transfers between devices with their start and end apart: 5, of which 2 were waited for; matrix products, arithmetic and copies ran while one was open for 0% of the time, Pallas kernels for 3%

profile of v3, /device:TPU:1, one launch (start us, length us, event | category | flops | bytes accessed | tf_op | source)
XLA Modules:
  0.0 173.2 jit_solution(11132680606352623671)
XLA Ops:
  0.0 19.4 %all_gather.18.refs_3_ = f32[192,1024]{1,0:T(8,128)S(1)} all-gather(f32[48,1024]{1,0:T(8,128)} %bitcast.17), channel_id=1, replica_groups=mesh['y'=4,'zh'=4,'c'=2,'x'=4,'zl'=4] {'zl'}, dimensions={0}, use_global_device_ids=true | all-gather | bytes 983040 | tf_op jit(solution)/shard_map/all_gather | solution.py:190
  19.4 2.9 %collective-permute-start.1 = (f32[192,1024]{1,0:T(8,128)S(1)}, f32[192,1024]{1,0:T(8,128)S(1)}, u32[]{:S(2)}, u32[]{:S(2)}) collective-permute-start(f32[192,1024]{1,0:T(8,128)S(1)} %all_gather.18.refs_3_), channel_id=1, source_target_pairs={{0,4},{4,8},{8,12},{12,0},{1,5},{5,9},{9,13},{13,1},{2,6},{6,10},{... | collective-permute-start | bytes 2359304 | tf_op jit(solution)/shard_map/ppermute | solution.py:191
  22.4 3.6 %collective-permute-start = (f32[192,1024]{1,0:T(8,128)S(1)}, f32[192,1024]{1,0:T(8,128)S(1)}, u32[]{:S(2)}, u32[]{:S(2)}) collective-permute-start(f32[192,1024]{1,0:T(8,128)S(1)} %all_gather.18.refs_3_), channel_id=1, source_target_pairs={{0,12},{4,0},{8,4},{12,8},{1,13},{5,1},{9,5},{13,9},{2,14},{6,2},{... | collective-permute-start | bytes 2359304 | tf_op jit(solution)/shard_map/ppermute | solution.py:192
  25.9 3.3 %collective-permute-start.2 = (f32[48,1024]{1,0:T(8,128)}, f32[48,1024]{1,0:T(8,128)S(1)}, u32[]{:S(2)}, u32[]{:S(2)}) collective-permute-start(f32[48,1024]{1,0:T(8,128)} %bitcast.18), channel_id=1, source_target_pairs={{0,8},{4,12},{8,0},{12,4},{1,9},{5,13},{9,1},{13,5},{2,10},{6,14},... | collective-permute-start | bytes 589832 | tf_op jit(solution)/shard_map/ppermute | solution.py:189
  29.2 0.0 copy-start
  29.2 1.6 copy-done
  30.8 0.5 shard_map.28
  31.3 0.1 pad_add_fusion.where.refs_0_
  31.3 11.7 %collective-permute-done.2 = f32[48,1024]{1,0:T(8,128)S(1)} collective-permute-done((f32[48,1024]{1,0:T(8,128)}, f32[48,1024]{1,0:T(8,128)S(1)}, u32[]{:S(2)}, u32[]{:S(2)}) %collective-permute-start.2) | collective-permute-done | bytes 196640 | tf_op jit(solution)/shard_map/ppermute | solution.py:189
  43.1 16.2 %all_gather.19.refs_4_ = f32[192,1024]{1,0:T(8,128)S(1)} all-gather(f32[48,1024]{1,0:T(8,128)S(1)} %collective-permute-done.2), channel_id=1, replica_groups=mesh['y'=4,'zh'=4,'c'=2,'x'=4,'zl'=4] {'zl'}, dimensions={0}, use_global_device_ids=true | all-gather | bytes 983040 | tf_op jit(solution)/shard_map/all_gather | solution.py:194
  59.3 2.1 %shard_map.29 = (f32[512,192]{1,0:T(8,128)S(1)}, f32[2,192]{1,0:T(2,128)S(1)}, bf16[192,1024]{1,0:T(8,128)(2,1)S(1)}, bf16[192,1024]{1,0:T(8,128)(2,1)S(1)}, f32...) custom-call(bf16[512,1024]{1,0:T(8,128)(2,1)S(1)} %get-tuple-element., ...), custom_call_target="tpu_custom_call" | custom-call | flops 1207959552 | bytes 4194304 | tf_op jit(solution)/shard_map/pallas_call | solution.py:87
  61.4 0.0 collective-permute-done.1.refs_4_
  61.4 0.0 collective-permute-done.refs_3_
  61.4 2.6 %shard_map.30 = (f32[512,192]{1,0:T(8,128)S(1)}, f32[2,192]{1,0:T(2,128)S(1)}, bf16[192,1024]{1,0:T(8,128)(2,1)S(1)}, bf16[192,1024]{1,0:T(8,128)(2,1)S(1)}, f32...) custom-call(s32[3]{0:T(128)S(1)} %pad_add_fusion.where.refs_0_, ...), custom_call_target="tpu_custom_call" | custom-call | flops 1207959552 | bytes 4194304 | tf_op jit(solution)/shard_map/pallas_call | solution.py:104
  64.0 13.7 %all_to_all.15.refs_1_ = f32[16,4,2,192]{3,2,1,0:T(2,128)S(1)} all-to-all(f32[16,4,2,192]{3,2,1,0:T(2,128)S(1)} %get-tuple-element.46), channel_id=1, replica_groups=mesh['y'=4,'zh'=4,'c'=2,'x'=4,'zl'=4] {'x','zl'}, dimensions={0} | all-to-all | bytes 196608 | tf_op jit(solution)/shard_map/all_to_all | solution.py:202
  77.7 2.4 %shard_map.31 = (f32[4,65,8,128]{3,2,1,0:T(8,128)S(1)}, f32[4,192]{1,0:T(4,128)S(1)}) custom-call(s32[3]{0:T(128)S(1)} %pad_add_fusion.where.refs_0_, f32[16,4,2,192]{3,2,1,0:T(2,128)S(1)} %all_to_all.15.refs_1_, f32[512,192]{1,0:T(8,128)S(1)} %get-tuple-element.47.refs_2_, f32[2,192]{1,0:T(2,128)S(1)} %get-tuple-element.44.refs_5_.refs_3_, ...), custom_call_target="tpu_custom_call" | custom-call | flops 1207959552 | bytes 4194304 | tf_op jit(solution)/shard_map/pallas_call | solution.py:146
  80.1 8.7 %collective-permute-start.3 = (f32[4,65,8,128]{3,2,1,0:T(8,128)S(1)}, f32[4,65,8,128]{3,2,1,0:T(8,128)S(1)}, u32[]{:S(2)}, u32[]{:S(2)}) collective-permute-start(f32[4,65,8,128]{3,2,1,0:T(8,128)S(1)} %get-tuple-element.62), channel_id=1, source_target_pairs={{0,16},{16,0},{1,17},{17,1},{2,18},{18,2},{3,19},{19,3},{4,20},{20... | collective-permute-start | bytes 3194888 | tf_op jit(solution)/shard_map/ppermute | solution.py:205
  88.8 2.3 %shard_map.32 = f32[4,65,8,128]{3,2,1,0:T(8,128)S(1)} custom-call(s32[3]{0:T(128)S(1)} %pad_add_fusion.where.refs_0_, f32[4,192]{1,0:T(4,128)S(1)} %get-tuple-element.61.refs_1_, f32[512,192]{1,0:T(8,128)S(1)} %get-tuple-element.47.refs_2_, f32[2,192]{1,0:T(2,128)S(1)} %get-tuple-element.44.refs_5_.refs_3_, bf16[192,1024]{1,0:T(8,128)(2,1)S(1)} %get-tuple-element.48.refs_4_, ...), custom_call_target="tpu_custom_call" | custom-call | flops 1207959552 | bytes 4194304 | tf_op jit(solution)/shard_map/pallas_call | solution.py:146
  91.2 0.0 collective-permute-done.3
  91.2 0.1 add.7
  91.3 19.2 %all_to_all.16.parts = f32[4,65,8,128]{3,2,1,0:T(8,128)S(1)} all-to-all(f32[4,65,8,128]{3,2,1,0:T(8,128)S(1)} %add.7), channel_id=1, replica_groups=mesh['y'=4,'zh'=4,'c'=2,'x'=4,'zl'=4] {'y'}, dimensions={0} | all-to-all | bytes 2129920 | tf_op jit(solution)/shard_map/all_to_all | solution.py:207
  110.5 0.0 copy-start.1
  110.6 20.6 %all-gather = f32[130,8,128]{2,1,0:T(8,128)S(1)} all-gather(f32[65,8,128]{2,1,0:T(8,128)S(1)} %shard_map.33), channel_id=2, replica_groups={{0,32},{64,96},{48,80},{112,16},{1,33},{65,97},{49,81},{113,17},{2,34},..., dimensions={0}, use_global_device_ids=true | all-gather | bytes 798720 | tf_op jit(solution)/shard_map/all_gather | solution.py:208
  131.2 17.1 %all-gather.1 = f32[130,8,128]{2,1,0:T(8,128)S(1)} all-gather(f32[65,8,128]{2,1,0:T(8,128)S(1)} %shard_map.34), channel_id=3, replica_groups={{32,64},{96,0},{16,48},{80,112},{33,65},{97,1},{17,49},{81,113},{34,66}..., dimensions={0}, use_global_device_ids=true | all-gather | bytes 798720 | tf_op jit(solution)/shard_map/all_gather | solution.py:209
  148.3 0.0 copy-done.1
  148.3 0.7 shard_map.35
  149.0 15.8 %all_to_all.17 = f32[4,64,8,128]{3,2,1,0:T(8,128)S(1)} all-to-all(f32[4,64,8,128]{3,2,1,0:T(8,128)S(1)} %shard_map.35), channel_id=1, replica_groups=mesh['y'=4,'zh'=4,'c'=2,'x'=4,'zl'=4] {'y'}, dimensions={0} | all-to-all | bytes 2097152 | tf_op jit(solution)/shard_map/all_to_all | solution.py:211
  164.9 4.5 %collective-permute-start.4 = (f32[4,64,8,128]{3,2,1,0:T(8,128)S(1)}, f32[4,64,8,128]{3,2,1,0:T(8,128)S(1)}, u32[]{:S(2)}, u32[]{:S(2)}) collective-permute-start(f32[4,64,8,128]{3,2,1,0:T(8,128)S(1)} %all_to_all.17), channel_id=1, source_target_pairs={{0,16},{16,0},{1,17},{17,1},{2,18},{18,2},{3,19},{19,3},{4,20},{20... | collective-permute-start | bytes 3145736 | tf_op jit(solution)/shard_map/ppermute | solution.py:212
  169.4 2.3 %collective-permute-done.4 = f32[4,64,8,128]{3,2,1,0:T(8,128)S(1)} collective-permute-done((f32[4,64,8,128]{3,2,1,0:T(8,128)S(1)}, f32[4,64,8,128]{3,2,1,0:T(8,128)S(1)}, u32[]{:S(2)}, u32[]{:S(2)}) %collective-permute-start.4) | collective-permute-done | bytes 1048608 | tf_op jit(solution)/shard_map/ppermute | solution.py:212
  171.7 1.5 maximum_select_fusion
  (2 shorter events, 0.1 us)
Async XLA Ops:
  19.4 41.9 %collective-permute-start.1 = (f32[192,1024]{1,0:T(8,128)S(1)}, f32[192,1024]{1,0:T(8,128)S(1)}, u32[]{:S(2)}, u32[]{:S(2)}) collective-permute-start(f32[192,1024]{1,0:T(8,128)S(1)} %all_gather.18.refs_3_), channel_id=1, source_target_pairs={{0,4},{4,8},{8,12},{12,0},{1,5},{5,9},{9,13},{13,1},{2,6},{6,10},{... | collective-permute-start | bytes 2359304 | tf_op jit(solution)/shard_map/ppermute | solution.py:191
  22.4 39.0 %collective-permute-start = (f32[192,1024]{1,0:T(8,128)S(1)}, f32[192,1024]{1,0:T(8,128)S(1)}, u32[]{:S(2)}, u32[]{:S(2)}) collective-permute-start(f32[192,1024]{1,0:T(8,128)S(1)} %all_gather.18.refs_3_), channel_id=1, source_target_pairs={{0,12},{4,0},{8,4},{12,8},{1,13},{5,1},{9,5},{13,9},{2,14},{6,2},{... | collective-permute-start | bytes 2359304 | tf_op jit(solution)/shard_map/ppermute | solution.py:192
  25.9 17.1 %collective-permute-start.2 = (f32[48,1024]{1,0:T(8,128)}, f32[48,1024]{1,0:T(8,128)S(1)}, u32[]{:S(2)}, u32[]{:S(2)}) collective-permute-start(f32[48,1024]{1,0:T(8,128)} %bitcast.18), channel_id=1, source_target_pairs={{0,8},{4,12},{8,0},{12,4},{1,9},{5,13},{9,1},{13,5},{2,10},{6,14},... | collective-permute-start | bytes 589832 | tf_op jit(solution)/shard_map/ppermute | solution.py:189
  29.2 1.6 copy-start
  80.1 11.1 %collective-permute-start.3 = (f32[4,65,8,128]{3,2,1,0:T(8,128)S(1)}, f32[4,65,8,128]{3,2,1,0:T(8,128)S(1)}, u32[]{:S(2)}, u32[]{:S(2)}) collective-permute-start(f32[4,65,8,128]{3,2,1,0:T(8,128)S(1)} %get-tuple-element.62), channel_id=1, source_target_pairs={{0,16},{16,0},{1,17},{17,1},{2,18},{18,2},{3,19},{19,3},{4,20},{20... | collective-permute-start | bytes 3194888 | tf_op jit(solution)/shard_map/ppermute | solution.py:205
  110.5 37.8 %copy-start.1 = (f32[512,1024]{1,0:T(8,128)S(1)}, f32[512,1024]{1,0:T(8,128)}, u32[]{:S(2)}) copy-start(f32[512,1024]{1,0:T(8,128)} %views.3) | copy-start | bytes 6291460
  164.9 6.8 %collective-permute-start.4 = (f32[4,64,8,128]{3,2,1,0:T(8,128)S(1)}, f32[4,64,8,128]{3,2,1,0:T(8,128)S(1)}, u32[]{:S(2)}, u32[]{:S(2)}) collective-permute-start(f32[4,64,8,128]{3,2,1,0:T(8,128)S(1)} %all_to_all.17), channel_id=1, source_target_pairs={{0,16},{16,0},{1,17},{17,1},{2,18},{18,2},{3,19},{19,3},{4,20},{20... | collective-permute-start | bytes 3145736 | tf_op jit(solution)/shard_map/ppermute | solution.py:212
